TPU v7x, 768 devices: a whole 4x8x12 slice. The times are simulated.
768 devices in a mesh: dp: 128 (over z_hi, x, y), space: 6 (over z_lo, core).
Axes of the slice: x: 4, y: 8, z: 12 (z_hi: 4, z_lo: 3; z = z_hi * 3 + z_lo), core: 2. Of those that a mesh axis runs over, the one named last changes fastest.
Arguments:
- fields: bfloat16 [128, 126, 252, 192], P('dp', 'space'), may hold values from -6 to 6
- cotangent: bfloat16 [128, 126, 252, 192], P('dp', 'space'), may hold values from -1.796875 to 1.796875
- spec_real: bfloat16 [126, 192], replicated, may hold values from -4.1875 to 4.1875
- spec_imag: bfloat16 [126, 192], replicated, may hold values from -4.1875 to 4.1875
Outputs:
- grad_real: float32 [126, 192], replicated
- grad_imag: float32 [126, 192], replicated
All inputs are finite; a program needn't handle non-finite values.
Results may differ from a plain program's by a relative error of at most 0.015.
Values may be sent and summed in bfloat16 or wider, within the bound.
A program may use at most 64 MiB of HBM per device.

v0:
```python
import math

import jax
import jax.numpy as jnp
from jax import lax
from jax.sharding import PartitionSpec as P

NLAT = 126
NLON = 252
MODES = 126


def grid_tables():
    latitude = jnp.arange(NLAT, dtype=jnp.float32)
    colatitude = math.pi * (latitude + 0.5) / NLAT
    sin_theta = jnp.sin(colatitude)
    quad_weight = math.pi / NLAT * (2.0 * math.pi / NLON) * sin_theta
    return (jnp.cos(colatitude), sin_theta, quad_weight)


def fourier_tables(orders):
    longitude = jnp.arange(NLON, dtype=jnp.int32)
    phase_index = orders[:, None] * longitude[None, :] % NLON
    angles = 2.0 * math.pi / NLON * phase_index.astype(jnp.float32)
    basis_rows = jnp.stack([jnp.cos(angles), -jnp.sin(angles)], axis=1)
    factor = jnp.where(orders == 0, 1.0, 2.0).astype(jnp.float32)
    return (
        basis_rows.astype(jnp.bfloat16),
        (basis_rows * factor[:, None, None]).astype(jnp.bfloat16),
    )


def legendre(orders, cos_theta, sin_theta):
    counters = jnp.arange(1, MODES, dtype=jnp.float32)
    log_steps = 0.5 * jnp.log((2.0 * counters + 1.0) / (2.0 * counters))
    log_table = jnp.concatenate([jnp.zeros((1,), jnp.float32), jnp.cumsum(log_steps)])
    order_float = orders.astype(jnp.float32)[:, None]
    log_diagonal = (
        0.5 * jnp.log(1.0 / (4.0 * math.pi))
        + log_table[orders][:, None]
        + order_float * jnp.log(sin_theta)[None, :]
    )
    diagonal_start = jnp.exp(log_diagonal)
    cos_row = cos_theta[None, :]

    def advance(state_pair, degree):
        previous, earlier = state_pair
        degree_float = degree.astype(jnp.float32)
        growth = jnp.sqrt(
            jnp.maximum(4.0 * degree_float * degree_float - 1.0, 0.0)
            / jnp.maximum(degree_float * degree_float - order_float * order_float, 1.0)
        )
        below = degree_float - 1.0
        damping = jnp.sqrt(
            jnp.maximum(below * below - order_float * order_float, 0.0)
            / jnp.maximum(4.0 * below * below - 1.0, 1.0)
        )
        recurrence = growth * (cos_row * previous - damping * earlier)
        current = jnp.where(
            degree_float == order_float,
            diagonal_start,
            jnp.where(degree_float > order_float, recurrence, 0.0),
        )
        return ((current, previous), current)

    empty_rows = jnp.zeros_like(diagonal_start)
    final_state, stacked = lax.scan(
        advance, (empty_rows, empty_rows), jnp.arange(MODES, dtype=jnp.int32), unroll=6
    )
    return jnp.swapaxes(stacked, 0, 1)


def gelu_slope(values):
    cumulative = 0.5 * (1.0 + lax.erf(values / math.sqrt(2.0)))
    density = jnp.exp(-0.5 * values * values) / math.sqrt(2.0 * math.pi)
    return cumulative + values * density


def block_analysis(tables, coeffs):
    return jnp.einsum("qlj,sqjc->sqlc", tables, coeffs, preferred_element_type=jnp.float32)


def block_synthesis(tables, spectral):
    return jnp.einsum("qlj,sqlc->sqjc", tables, spectral, preferred_element_type=jnp.float32)


def apply_filter(spectral, real_rows, imag_rows):
    channels = real_rows.shape[-1]
    spec_values = spectral.astype(jnp.float32)
    real_part = spec_values[..., :channels]
    imag_part = spec_values[..., channels:]
    return jnp.concatenate(
        [
            real_part * real_rows - imag_part * imag_rows,
            real_part * imag_rows + imag_part * real_rows,
        ],
        axis=-1,
    ).astype(jnp.bfloat16)


def row_products(spectral, back_spectral):
    channels = spectral.shape[-1] // 2
    spec_values = spectral.astype(jnp.float32)
    back_values = back_spectral.astype(jnp.float32)
    real_term = (
        spec_values[..., :channels] * back_values[..., :channels]
        + spec_values[..., channels:] * back_values[..., channels:]
    )
    imag_term = (
        spec_values[..., :channels] * back_values[..., channels:]
        - spec_values[..., channels:] * back_values[..., :channels]
    )
    return (real_term, imag_term)


def grid_to_modes(grid_values, basis):
    cosine_part = jnp.einsum(
        "salc,ml->smac", grid_values, basis[:, 0], preferred_element_type=jnp.float32
    ).astype(jnp.bfloat16)
    sine_part = jnp.einsum(
        "salc,ml->smac", grid_values, basis[:, 1], preferred_element_type=jnp.float32
    ).astype(jnp.bfloat16)
    return jnp.concatenate([cosine_part, sine_part], axis=-1)


def modes_to_grid(mode_values, basis):
    channels = mode_values.shape[-1] // 2
    cosine_part = jnp.einsum(
        "smac,ml->salc",
        mode_values[..., :channels],
        basis[:, 0],
        preferred_element_type=jnp.float32,
    )
    sine_part = jnp.einsum(
        "smac,ml->salc",
        mode_values[..., channels:],
        basis[:, 1],
        preferred_element_type=jnp.float32,
    )
    return cosine_part + sine_part


def to_orders(grid_coeffs):
    return lax.all_to_all(grid_coeffs, "space", split_axis=1, concat_axis=2, tiled=True)


def on_device(fields, cotangent, spec_real, spec_imag):
    space_parts = lax.axis_size("space")
    band_index = lax.axis_index("space")
    slot_count = MODES // space_parts
    positions = jnp.arange(MODES, dtype=jnp.int32)
    slot_range = jnp.arange(slot_count, dtype=jnp.int32)
    local_orders = band_index * slot_count + slot_range
    forward_basis, inverse_basis = fourier_tables(positions)
    cos_theta, sin_theta, quad_weight = grid_tables()
    associated = legendre(local_orders, cos_theta, sin_theta)
    weighted = (associated * quad_weight[None, None, :]).astype(jnp.bfloat16)
    plain = associated.astype(jnp.bfloat16)
    real_rows = spec_real.astype(jnp.float32)
    imag_rows = spec_imag.astype(jnp.float32)

    def degree_sums(term):
        return jnp.sum(term, axis=(0, 1))

    coeffs = grid_to_modes(fields, forward_basis)
    by_order = to_orders(coeffs)
    spectral = block_analysis(weighted, by_order).astype(jnp.bfloat16)
    mixed = apply_filter(spectral, real_rows, imag_rows)
    synthesized = block_synthesis(plain, mixed).astype(jnp.bfloat16)
    by_band = lax.all_to_all(synthesized, "space", split_axis=2, concat_axis=1, tiled=True)
    signal = modes_to_grid(by_band, inverse_basis)
    upstream = (cotangent.astype(jnp.float32) * gelu_slope(signal)).astype(jnp.bfloat16)
    back_coeffs = grid_to_modes(upstream, inverse_basis)
    back_order = to_orders(back_coeffs)
    back_spectral = block_analysis(plain, back_order).astype(jnp.bfloat16)
    real_term, imag_term = row_products(spectral, back_spectral)
    part_real = degree_sums(real_term)
    part_imag = degree_sums(imag_term)
    summed_real, summed_imag = lax.psum((part_real, part_imag), ("dp", "space"))
    batch_total = fields.shape[0] * lax.axis_size("dp")
    return (summed_real / batch_total, summed_imag / batch_total)


def solution(mesh):
    in_specs = (P("dp", "space", None, None), P("dp", "space", None, None), P(), P())
    out_specs = (P(), P())
    return jax.shard_map(
        on_device, mesh=mesh, in_specs=in_specs, out_specs=out_specs, check_vma=False
    )
```

profile of v0, /device:TPU:1, one launch (start us, length us, event | category | flops | bytes accessed | tf_op | source)
XLA Modules:
  0.0 759.7 jit_solution(9613600461840506454)
XLA Ops:
  7.8 1.0 copy-done
  9.4 0.7 fusion.50
  11.1 2.8 copy.23
  13.9 14.0 %all-to-all-start = ((bf16[1,126,21,384]{3,2,0,1:T(8,128)(2,1)}), bf16[1,126,21,384]{3,2,0,1:T(8,128)(2,1)S(1)}, u32[]{:S(2)}, u32[]{:S(2)}) async-start(bf16[1,126,21,384]{3,2,0,1:T(8,128)(2,1)} %copy.23), calls=%async_computation | async-start | bytes 4644864 | tf_op jit(solution)/shard_map/all_to_all | solution.py:144
  28.4 0.7 gather_fusion
  29.2 126.3 %while.21 = (s32[]{:T(128)}, f32[21,126]{1,0:T(8,128)S(1)}, f32[21,126]{1,0:T(8,128)S(1)}, f32[21,6,21,126]{3,2,1,0:T(8,128)}, s32[21,6]{0,1:T(8,128)S(1)}, /*in...) while((s32[]{:T(128)}, f32[21,126]{1,0:T(8,128)S(1)}, ...), condition=%wide.region_2.3_spmd.clone.clone.clone.clone, body=%wide.region_1.2_spmd.clone.clone.clone.clone.sunk | while | flops 298316 | bytes 447497 | solution.py:67
  156.4 2.1 reshape.593
  158.6 2.8 convert_bitcast_fusion.1
  162.0 1.4 copy-done.2
  163.4 2.1 convert_bitcast_fusion.2
  165.5 2.8 copy.29
  168.4 4.2 all-to-all-start.1
  172.6 0.8 multiply_convert_fusion.1
  173.3 35.6 %all-to-all-done.1 = bf16[1,21,126,384]{3,1,0,2:T(8,128)(2,1)S(1)} async-done(((bf16[1,21,126,384]{3,1,0,2:T(8,128)(2,1)}), bf16[1,21,126,384]{3,1,0,2:T(8,128)(2,1)S(1)}, u32[]{:S(2)}, u32[]{:S(2)}) %all-to-all-start.1) | async-done | bytes 2032160 | tf_op jit(solution)/shard_map/all_to_all | solution.py:170
  209.3 1.9 copy.31
  211.2 2.7 all_to_all.41
  213.9 1.8 fusion.62
  215.7 2.0 copy.44
  217.7 1.7 copy.43
  219.4 1.6 fusion.52
  221.7 0.9 copy-done.4
  222.6 2.0 fusion.22
  225.3 0.7 fusion.51
  226.4 1.8 pad_maximum_fusion.1
  228.2 3.2 copy.34
  231.4 39.5 %all_to_all.48 = bf16[1,126,21,384]{3,2,0,1:T(8,128)(2,1)S(1)} all-to-all(bf16[1,126,21,384]{3,2,0,1:T(8,128)(2,1)S(1)} %copy.34), channel_id=1, replica_groups=mesh['dp'=128,'space'=6] {'space'}, dimensions={1} | all-to-all | bytes 4064256 | tf_op jit(solution)/shard_map/all_to_all | solution.py:144
  271.8 2.2 reshape.602
  273.9 2.9 convert_bitcast_fusion
  277.2 1.6 subtract_reduce_fusion
  278.8 471.0 %all-reduce.3.cloned.1.call-done = (f32[126,192]{0,1:T(8,128)}, f32[126,192]{0,1:T(8,128)}) async-done(((f32[126,192]{0,1:T(8,128)}, f32[126,192]{0,1:T(8,128)}), (f32[126,192]{0,1:T(8,128)}, f32[126,192]{0,1:T(8,128)})) %all-reduce.3.cloned.1.call-update) | async-done | bytes 193552 | tf_op jit(solution)/shard_map/psum | solution.py:179
  749.8 1.5 broadcast_multiply_fusion.1
  751.4 1.5 broadcast_multiply_fusion
  (511 shorter events, 52.8 us)
Async XLA Ops:
  7.2 1.6 copy-start
  13.9 141.7 %all-to-all-start = ((bf16[1,126,21,384]{3,2,0,1:T(8,128)(2,1)}), bf16[1,126,21,384]{3,2,0,1:T(8,128)(2,1)S(1)}, u32[]{:S(2)}, u32[]{:S(2)}) async-start(bf16[1,126,21,384]{3,2,0,1:T(8,128)(2,1)} %copy.23), calls=%async_computation | async-start | bytes 4644864 | tf_op jit(solution)/shard_map/all_to_all | solution.py:144
  29.1 126.3 %copy-start.6 = (bf16[126,192]{0,1:T(8,128)(2,1)S(1)}, bf16[126,192]{0,1:T(8,128)(2,1)}, u32[]{:S(2)}) copy-start(bf16[126,192]{0,1:T(8,128)(2,1)} %param.8) | copy-start | bytes 145156
  29.1 126.3 %copy-start.7 = (bf16[126,192]{0,1:T(8,128)(2,1)S(1)}, bf16[126,192]{0,1:T(8,128)(2,1)}, u32[]{:S(2)}) copy-start(bf16[126,192]{0,1:T(8,128)(2,1)} %param.9) | copy-start | bytes 145156
  161.4 2.0 copy-start.2
  168.4 40.6 %all-to-all-start.1 = ((bf16[1,21,126,384]{3,1,0,2:T(8,128)(2,1)}), bf16[1,21,126,384]{3,1,0,2:T(8,128)(2,1)S(1)}, u32[]{:S(2)}, u32[]{:S(2)}) async-start(bf16[1,21,126,384]{3,1,0,2:T(8,128)(2,1)} %copy.29), calls=%async_computation.1 | async-start | bytes 4644864 | tf_op jit(solution)/shard_map/all_to_all | solution.py:170
  172.6 577.3 %all-reduce.3.cloned.1.call-start = ((), (), s32[]{:S(2)}) async-start(), calls=%async_computation.3 | async-start | bytes 393216 | tf_op jit(solution)/shard_map/psum | solution.py:179
  219.4 1.6 copy-start.5
  221.0 1.6 copy-start.4
  273.9 3.3 copy-start.3
  277.2 475.7 %copy-start.1 = (bf16[1,21,252,192]{2,3,1,0:T(8,128)(2,1)S(1)}, bf16[1,21,252,192]{2,3,1,0:T(8,128)(2,1)}, u32[]{:S(2)}) copy-start(bf16[1,21,252,192]{2,3,1,0:T(8,128)(2,1)} %param.6) | copy-start | bytes 6096388
Sparse Core Ops, SparseCore 0:
  278.9 470.8 all-reduce.2
where the time goes:
time: 762 us; the launch traced here: 760 us
  waiting for transfers between devices  507 us (67%)
  loops' own time  81 us (11%)
  local copies, waits for them, and re-layouts  56.9 us (7%)
  blocking collectives  39.5 us (5%)
  other arithmetic  30.3 us (4%)
  starting transfers between devices  18.2 us (2%)
  between operations  14.4 us (2%)
  matrix products  12.9 us (2%)
    psum x1, waiting for transfers between devices, on_device(): summed_real, summed_imag = lax.psum((part_real, part_imag), ('dp', 'space'))  471 us
    another operation x1, loops' own time, legendre(): lax.scan(advance, (empty_rows, empty_rows), jnp.arange(MODES, dtype=jnp.i...  81 us
    all_to_all x1, blocking collectives, to_orders(): lax.all_to_all(grid_coeffs, 'space', split_axis=1, concat_axis=2, tiled=T...  39.5 us
    all_to_all x1, waiting for transfers between devices, on_device(): lax.all_to_all(synthesized, 'space', split_axis=2, concat_axis=1, tiled=T...  35.6 us
  transfers between devices with their start and end apart: 3, of which 2 were waited for; matrix products, arithmetic and copies ran while one was open for 6% of the time, Pallas kernels for 0%

commit v1 on v0

v1 whole, which is shorter than its diff:
```python
import functools
import math

import jax
import jax.numpy as jnp
import ml_dtypes
import numpy as np
from jax import lax
from jax.experimental import pallas as pl
from jax.experimental.pallas import tpu as pltpu
from jax.sharding import PartitionSpec as P

NLAT = 126
NLON = 252
MODES = 126
CHANNELS = 192
HALF = 63
PARTS = 6
BAND = 21
SLICE = 32
ROWS = 64
LANES = 128
MESH = pl.DeviceIdType.MESH
NT = (((1,), (1,)), ((), ()))
NN = (((1,), (0,)), ((), ()))


def legendre_table(theta):
    counters = np.arange(1, MODES, dtype=np.float64)
    steps = 0.5 * np.log((2.0 * counters + 1.0) / (2.0 * counters))
    log_table = np.concatenate([np.zeros(1), np.cumsum(steps)])
    orders = np.arange(MODES, dtype=np.float64)[:, None]
    diagonal = np.exp(
        0.5 * np.log(1.0 / (4.0 * math.pi))
        + log_table[:, None]
        + orders * np.log(np.sin(theta))[None, :]
    )
    cosine = np.cos(theta)[None, :]
    previous = np.zeros_like(diagonal)
    earlier = np.zeros_like(diagonal)
    table = np.zeros((MODES, MODES, theta.size))
    for degree in range(MODES):
        growth = np.sqrt(
            max(4.0 * degree * degree - 1.0, 0.0)
            / np.maximum(degree * degree - orders * orders, 1.0)
        )
        below = degree - 1.0
        damping = np.sqrt(
            np.maximum(below * below - orders * orders, 0.0)
            / max(4.0 * below * below - 1.0, 1.0)
        )
        current = growth * (cosine * previous - damping * earlier)
        current = np.where(
            orders == degree, diagonal, np.where(orders < degree, current, 0.0)
        )
        table[:, degree] = current
        previous, earlier = current, previous
    return table


def tables():
    theta = math.pi * (np.arange(HALF) + 0.5) / NLAT
    weight = np.zeros(ROWS, np.float32)
    weight[:HALF] = math.pi / NLAT * (2.0 * math.pi / NLON) * np.sin(theta)
    plain = np.zeros((MODES, ROWS, LANES), np.float32)
    plain[:, :HALF, :MODES] = legendre_table(theta).transpose(0, 2, 1)
    orders = np.arange(MODES)
    phase = orders[:, None] * np.arange(NLON)[None, :] % NLON
    angles = 2.0 * math.pi / NLON * phase
    basis = np.zeros((2, LANES, NLON), np.float32)
    basis[0, :MODES] = np.cos(angles)
    basis[1, :MODES] = -np.sin(angles)
    factor = np.full((LANES, 1), 2.0, np.float32)
    factor[0] = 1.0
    forward = basis.astype(ml_dtypes.bfloat16)
    inverse = (forward.astype(np.float32) * factor).astype(ml_dtypes.bfloat16)
    return weight, plain.astype(ml_dtypes.bfloat16), forward, inverse


def gelu_slope(values):
    cumulative = 0.5 * (1.0 + lax.erf(values * (1.0 / math.sqrt(2.0))))
    density = jnp.exp(-0.5 * values * values) * (1.0 / math.sqrt(2.0 * math.pi))
    return cumulative + values * density


def dot(a, b, dims=NN):
    return lax.dot_general(a, b, dims, preferred_element_type=jnp.float32)


def kernel(
    grid_dims,
    scale,
    weight_ref,
    fields_ref,
    cot_ref,
    plain_hbm,
    forward_ref,
    inverse_ref,
    real_ref,
    imag_ref,
    out_real,
    out_imag,
    field,
    cot,
    plain,
    turned,
    work,
    slope,
    spec,
    swap,
    filt,
    acc,
    packed,
    xbuf,
    ybuf,
    zbuf,
    mine,
    gathered,
    local_sem,
    send_f,
    recv_f,
    send_c,
    recv_c,
    send_x,
    recv_x,
    send_y,
    recv_y,
    send_z,
    recv_z,
    send_s,
    recv_s,
    send_g,
    recv_g,
):
    n_z, n_x, n_y = grid_dims
    rows = ROWS // n_x
    me = lax.axis_index("space")
    dp = lax.axis_index("dp")
    zi = dp // (n_x * n_y)
    xi = lax.rem(dp // n_y, n_x)
    yi = lax.rem(dp, n_y)
    chip, core = me // 2, lax.rem(me, 2)
    first = jnp.where(chip == 0, 2, 0)
    second = 3 - chip - first
    space_peers = [
        2 * first + core,
        2 * first + 1 - core,
        2 * second + core,
        2 * second + 1 - core,
        2 * chip + 1 - core,
    ]
    x_peers = [lax.rem(xi + r, n_x) for r in range(1, n_x)]
    y_peers = [lax.rem(yi + r, n_y) for r in range(1, n_y)]
    z_peers = [lax.rem(zi + r, n_z) for r in range(1, n_z)]

    def at_x(x):
        return {"dp": (zi * n_x + x) * n_y + yi}

    def at_y(y):
        return {"dp": (zi * n_x + xi) * n_y + y}

    def at_z(z):
        return {"dp": (z * n_x + xi) * n_y + yi}

    everyone = (
        [{"space": s} for s in space_peers]
        + [at_x(x) for x in x_peers]
        + [at_y(y) for y in y_peers]
        + [at_z(z) for z in z_peers]
    )
    barrier = pltpu.get_barrier_semaphore()
    for target in everyone:
        pl.semaphore_signal(barrier, inc=1, device_id=target, device_id_type=MESH)

    load = pltpu.make_async_copy(plain_hbm, plain, local_sem.at[0])
    load.start()
    mine_lanes = pl.ds(pl.multiple_of(me * SLICE, SLICE), SLICE)
    own_f = pltpu.make_async_copy(
        fields_ref.at[:, mine_lanes, :], field.at[pl.ds(me * BAND, BAND)], recv_f.at[me]
    )
    own_c = pltpu.make_async_copy(
        cot_ref.at[:, mine_lanes, :], cot.at[pl.ds(me * BAND, BAND)], recv_c.at[me]
    )
    own_f.start()
    own_c.start()
    pl.semaphore_wait(barrier, len(everyone))

    def exchange(source, target, send, recv):
        copies = []
        for slot, peer in enumerate(space_peers):
            lanes = pl.ds(pl.multiple_of(peer * SLICE, SLICE), SLICE)
            copies.append(
                pltpu.make_async_remote_copy(
                    src_ref=source.at[:, lanes, :],
                    dst_ref=target.at[pl.ds(me * BAND, BAND)],
                    send_sem=send.at[slot],
                    recv_sem=recv.at[me],
                    device_id={"space": peer},
                    device_id_type=MESH,
                )
            )
            copies[-1].start()
        return copies

    sends = exchange(fields_ref, field, send_f, recv_f)
    sends += exchange(cot_ref, cot, send_c, recv_c)

    def arrive(target, recv, band):
        block = target.at[pl.ds(band * BAND, BAND)]
        pltpu.make_async_copy(block, block, recv.at[band]).wait()

    for index, source in enumerate((real_ref, imag_ref)):
        filt[index] = jnp.zeros((LANES, LANES), jnp.float32)
        values = source[mine_lanes, :].astype(jnp.float32)
        filt[index, :, :MODES] = jnp.concatenate([values] * 4, axis=0)
        filt[index] = filt[index].T
    work[pl.ds(HALF, LANES, stride=ROWS), :] = jnp.zeros((LANES, LANES), jnp.float32)
    load.wait()

    @pl.loop(0, MODES)
    def _(m):
        turned[m] = plain[m].astype(jnp.float32).T.astype(jnp.bfloat16)

    zero = jnp.zeros((SLICE, NLON), jnp.bfloat16)

    def to_modes(north, south, basis_ref, j, factor):
        cosine = jnp.concatenate([north, zero, south, zero], axis=0)
        sine = jnp.concatenate([zero, north, zero, south], axis=0)
        modes = dot(basis_ref[0], cosine, NT) + dot(basis_ref[1], sine, NT)
        if factor is not None:
            modes = modes * factor
        work[pl.ds(j, LANES, stride=ROWS), :] = modes

    for band in (2, 1, 0):
        arrive(field, recv_f, band)
        arrive(field, recv_f, PARTS - 1 - band)

        @pl.loop(0, BAND)
        def _(t, band=band):
            j = band * BAND + t
            to_modes(
                field[j], field[NLAT - 1 - j], forward_ref, j, weight_ref[j]
            )

    lane = lax.broadcasted_iota(jnp.int32, (8, LANES), 1)
    odd_group = (lax.rem(lane // SLICE, 2) == 1)[None]
    degree = lax.broadcasted_iota(jnp.int32, (8, LANES), 0)
    sign = (1 - 2 * lax.rem(degree, 2)).astype(jnp.float32)[None]

    for group in range(8):
        low = 16 * group
        depth = LANES - low
        pairs = (min(16, MODES - low)) // 2

        @pl.loop(0, pairs)
        def _(i, low=low, depth=depth):
            for odd in (0, 1):
                m = low + 2 * i + odd
                at = pl.ds(pl.multiple_of(m * ROWS, ROWS), ROWS)
                part = dot(turned[m, low:, :], work[at, :].astype(jnp.bfloat16))
                other = pltpu.roll(part, 2 * SLICE, 1)
                part = part.reshape(depth // 8, 8, LANES)
                other = other.reshape(depth // 8, 8, LANES) * sign
                full = part - other if odd else part + other
                rounded = full.reshape(depth, LANES).astype(jnp.bfloat16)
                values = rounded.astype(jnp.float32)
                left = pltpu.roll(values, LANES - SLICE, 1).reshape(depth // 8, 8, LANES)
                right = pltpu.roll(values, SLICE, 1).reshape(depth // 8, 8, LANES)
                turn = jnp.where(odd_group, right, -left).reshape(depth, LANES)
                spec[m, low:, :] = rounded
                swap[m, low:, :] = turn.astype(jnp.bfloat16)
                mixed = values * filt[0, low:, :] + turn * filt[1, low:, :]
                mixed = mixed.astype(jnp.bfloat16)
                if low:
                    mixed = jnp.concatenate(
                        [jnp.zeros((low, LANES), jnp.bfloat16), mixed], axis=0
                    )
                work[at, :] = dot(plain[m], mixed)

    @pl.loop(0, HALF)
    def _(j):
        modes = work[pl.ds(j, LANES, stride=ROWS), :].T.astype(jnp.bfloat16)
        cosine = jnp.concatenate(
            [modes[:SLICE], modes[2 * SLICE : 3 * SLICE]], axis=0
        )
        sine = jnp.concatenate([modes[SLICE : 2 * SLICE], modes[3 * SLICE :]], axis=0)
        signal = dot(cosine, inverse_ref[0]) + dot(sine, inverse_ref[1])
        slope[j] = gelu_slope(signal)

    for band in (2, 1, 0):
        arrive(cot, recv_c, band)
        arrive(cot, recv_c, PARTS - 1 - band)

        @pl.loop(0, BAND)
        def _(t, band=band):
            j = band * BAND + t
            north = cot[j].astype(jnp.float32) * slope[j, :SLICE]
            south = cot[NLAT - 1 - j].astype(jnp.float32) * slope[j, SLICE:]
            to_modes(
                north.astype(jnp.bfloat16),
                south.astype(jnp.bfloat16),
                inverse_ref,
                j,
                None,
            )

    acc[...] = jnp.zeros_like(acc)
    for group in range(8):
        low = 16 * group
        pairs = (min(16, MODES - low)) // 2

        @pl.loop(0, pairs)
        def _(i, low=low):
            total = [acc[0, low:, :], acc[1, low:, :]]
            for odd in (0, 1):
                m = low + 2 * i + odd
                at = pl.ds(pl.multiple_of(m * ROWS, ROWS), ROWS)
                back = dot(turned[m, low:, :], work[at, :].astype(jnp.bfloat16))
                total[0] += back * spec[m, low:, :].astype(jnp.float32)
                total[1] += back * swap[m, low:, :].astype(jnp.float32)
            acc[0, low:, :] = total[0]
            acc[1, low:, :] = total[1]

    for index in range(2):
        total = acc[index].T * scale
        packed[pl.ds(index * SLICE, SLICE), :] = (
            total[:SLICE] + total[SLICE : 2 * SLICE]
        ) + (total[2 * SLICE : 3 * SLICE] + total[3 * SLICE :])

    def remote(src, dst, send, recv, target):
        copy = pltpu.make_async_remote_copy(
            src_ref=src,
            dst_ref=dst,
            send_sem=send,
            recv_sem=recv,
            device_id=target,
            device_id_type=MESH,
        )
        copy.start()
        return copy

    def piece(x):
        return pl.ds(pl.multiple_of(x * rows, rows), rows)

    copies = [
        remote(packed.at[piece(x)], xbuf.at[xi], send_x.at[r], recv_x.at[r], at_x(x))
        for r, x in enumerate(x_peers)
    ]
    xbuf[xi] = packed[piece(xi), :]
    for copy in copies:
        copy.wait()
    mine[0] = sum((xbuf[i] for i in range(1, n_x)), xbuf[0])

    copies = [
        remote(mine.at[0], ybuf.at[yi], send_y.at[r], recv_y.at[r], at_y(y))
        for r, y in enumerate(y_peers)
    ]
    ybuf[yi] = mine[0]
    for copy in copies:
        copy.wait()
    mine[1] = sum((ybuf[i] for i in range(1, n_y)), ybuf[0])

    copies = [
        remote(mine.at[1], zbuf.at[zi], send_z.at[r], recv_z.at[r], at_z(z))
        for r, z in enumerate(z_peers)
    ]
    zbuf[zi] = mine[1]
    for copy in copies:
        copy.wait()
    mine[2] = sum((zbuf[i] for i in range(1, n_z)), zbuf[0])

    spot = gathered.at[me, piece(xi)]
    copies = [
        remote(mine.at[2], spot, send_s.at[r], recv_s.at[me], {"space": s})
        for r, s in enumerate(space_peers)
    ]
    gathered[me, piece(xi)] = mine[2]
    for copy in copies:
        copy.wait_send()
    for s in space_peers:
        spot = gathered.at[s, piece(xi)]
        pltpu.make_async_copy(spot, spot, recv_s.at[s]).wait()

    column = gathered.at[:, piece(xi)]
    copies = [
        remote(column, column, send_g.at[r], recv_g.at[xi], at_x(x))
        for r, x in enumerate(x_peers)
    ]
    for copy in copies:
        copy.wait_send()
    for x in x_peers:
        spot = gathered.at[:, piece(x)]
        pltpu.make_async_copy(spot, spot, recv_g.at[x]).wait()

    for s in range(PARTS):
        out_real[s * SLICE : (s + 1) * SLICE, :] = gathered[s, :SLICE, :MODES]
        out_imag[s * SLICE : (s + 1) * SLICE, :] = gathered[s, SLICE:, :MODES]
    for copy in sends:
        copy.wait_send()


def on_device(grid_dims, batch, fields, cotangent, spec_real, spec_imag):
    n_z, n_x, n_y = grid_dims
    rows = ROWS // n_x
    weight, plain, forward, inverse = tables()
    fields = jnp.transpose(fields[0], (0, 2, 1))
    cotangent = jnp.transpose(cotangent[0], (0, 2, 1))
    vmem = pl.BlockSpec(memory_space=pltpu.VMEM)
    anywhere = pl.BlockSpec(memory_space=pl.ANY)
    out = jax.ShapeDtypeStruct((CHANNELS, MODES), jnp.float32)
    dma = pltpu.SemaphoreType.DMA
    result = pl.pallas_call(
        functools.partial(kernel, grid_dims, 1.0 / batch),
        out_shape=(out, out),
        in_specs=[
            pl.BlockSpec(memory_space=pltpu.SMEM),
            anywhere,
            anywhere,
            anywhere,
            vmem,
            vmem,
            vmem,
            vmem,
        ],
        out_specs=(vmem, vmem),
        scratch_shapes=[
            pltpu.VMEM((NLAT, SLICE, NLON), jnp.bfloat16),
            pltpu.VMEM((NLAT, SLICE, NLON), jnp.bfloat16),
            pltpu.VMEM((MODES, ROWS, LANES), jnp.bfloat16),
            pltpu.VMEM((MODES, LANES, ROWS), jnp.bfloat16),
            pltpu.VMEM((LANES * ROWS, LANES), jnp.float32),
            pltpu.VMEM((HALF, ROWS, NLON), jnp.float32),
            pltpu.VMEM((MODES, LANES, LANES), jnp.bfloat16),
            pltpu.VMEM((MODES, LANES, LANES), jnp.bfloat16),
            pltpu.VMEM((2, LANES, LANES), jnp.float32),
            pltpu.VMEM((2, LANES, LANES), jnp.float32),
            pltpu.VMEM((ROWS, LANES), jnp.float32),
            pltpu.VMEM((n_x, rows, LANES), jnp.float32),
            pltpu.VMEM((n_y, rows, LANES), jnp.float32),
            pltpu.VMEM((n_z, rows, LANES), jnp.float32),
            pltpu.VMEM((3, rows, LANES), jnp.float32),
            pltpu.VMEM((PARTS, ROWS, LANES), jnp.float32),
            dma((1,)),
            dma((PARTS,)),
            dma((PARTS,)),
            dma((PARTS,)),
            dma((PARTS,)),
            dma((n_x,)),
            dma((n_x,)),
            dma((n_y,)),
            dma((n_y,)),
            dma((n_z,)),
            dma((n_z,)),
            dma((PARTS,)),
            dma((PARTS,)),
            dma((n_x,)),
            dma((n_x,)),
        ],
        compiler_params=pltpu.CompilerParams(
            collective_id=0, has_side_effects=True, vmem_limit_bytes=56 * 2**20
        ),
    )(
        jnp.asarray(weight),
        fields,
        cotangent,
        jnp.asarray(plain),
        jnp.asarray(forward),
        jnp.asarray(inverse),
        spec_real.T,
        spec_imag.T,
    )
    return (result[0].T, result[1].T)


def solution(mesh):
    samples = mesh.shape["dp"]
    grid_dims = (4, 4, 8) if samples == 128 else (1, 1, 1)
    in_specs = (P("dp", "space", None, None), P("dp", "space", None, None), P(), P())
    return jax.shard_map(
        functools.partial(on_device, grid_dims, samples),
        mesh=mesh,
        in_specs=in_specs,
        out_specs=(P(), P()),
        check_vma=False,
    )
```

time: 762 us -> 164 us (0.22)
  waiting for transfers between devices: 507 us -> 0 us
  Pallas kernels: 0 us -> 160 us
  loops' own time: 81 us -> 0 us
  local copies, waits for them, and re-layouts: 56.9 us -> 3.08 us
  blocking collectives: 39.5 us -> 0 us
  other arithmetic: 30.3 us -> 0 us
  starting transfers between devices: 18.2 us -> 0 us
  between operations: 14.4 us -> 0.64 us
  matrix products: 12.9 us -> 0 us
    psum x1 -> x0, waiting for transfers between devices: 471 us -> none  [on_device(): summed_real, summed_imag = lax.psum((part_real, part_imag), ('dp', 'space'))]
    pallas_call x0 -> x1, Pallas kernels: none -> 160 us  [on_device(): pl.pallas_call(functools.partial(kernel, grid_dims, 1.0 / batch), out_sha...]
    another operation x1 -> x0, loops' own time: 81 us -> none  [legendre(): lax.scan(advance, (empty_rows, empty_rows), jnp.arange(MODES, dtype=jnp.i...]
    all_to_all x1 -> x0, blocking collectives: 39.5 us -> none  [to_orders(): lax.all_to_all(grid_coeffs, 'space', split_axis=1, concat_axis=2, tiled=T...]
    all_to_all x2 -> x0, waiting for transfers between devices: 35.6 us -> none  [the longest x1 35.6 us: on_device(): lax.all_to_all(synthesized, 'space', split_axis=2, concat_axis=1, tiled=T...]
    all_to_all x2 -> x0, starting transfers between devices: 18.2 us -> none  [the longest x1 14 us: to_orders(): lax.all_to_all(grid_coeffs, 'space', split_axis=1, concat_axis=2, tiled=T...]
    slice x22 -> x0, local copies, waits for them, and re-layouts: 14.1 us -> none  [the longest x21 12.3 us: legendre(): lax.scan(advance, (empty_rows, empty_rows), jnp.arange(MODES, dtype=jnp.i...]
    dynamic_update_slice x21 -> x0, local copies, waits for them, and re-layouts: 13.4 us -> none  [legendre(): lax.scan(advance, (empty_rows, empty_rows), jnp.arange(MODES, dtype=jnp.i...]
  transfers between devices with their start and end apart: 3 -> 0, of which waited for: 2 -> 0; matrix products, arithmetic and copies ran while one was open for 6% -> 0% of each run, Pallas kernels for 0% -> 0%
where the time goes in v1:
time: 164 us
  Pallas kernels  160 us (98%)
  local copies, waits for them, and re-layouts  3.08 us (2%)
    pallas_call x1, Pallas kernels, on_device(): pl.pallas_call(functools.partial(kernel, grid_dims, 1.0 / batch), out_sha...  160 us

profile of v1, /device:TPU:1, one launch (start us, length us, event | category | flops | bytes accessed | tf_op | source)
XLA Modules:
  0.0 164.1 jit_solution(575332690019765147)
XLA Ops:
  0.6 160.4 %shard_map.95 = (f32[192,126]{1,0:T(8,128)}, f32[192,126]{1,0:T(8,128)}) custom-call(f32[64]{0:T(128)} %constant.8.clone.weight_ref, bf16[21,192,252]{2,1,0:T(8,128)(2,1)} %bitcast.10, bf16[21,192,252]{2,1,0:T(8,128)(2,1)} %bitcast.11, bf16[126,64,128]{2,1,0:T(8,128)(2,1)} %constant.9.clone.plain_hbm, bf16[2,128,252]{2,1,0:T(8,128)(2,1)} %constant.10.clone.forward_ref, ...), custom_call_target="tpu_custom_call" | custom-call | tf_op jit(solution)/shard_map/pallas_call | solution.py:412
  161.0 1.5 copy.12
  162.6 1.5 copy.13

commit v2 on v1

--- a/solution.py
+++ b/solution.py
@@ -13,6 +13,7 @@
 NLAT = 126
 NLON = 252
 MODES = 126
+ORDERS = 128
 CHANNELS = 192
 HALF = 63
 PARTS = 6
@@ -20,6 +21,9 @@
 SLICE = 32
 ROWS = 64
 LANES = 128
+STEP = 3
+UNROLL = 4
+BACK_UNROLL = 8
 MESH = pl.DeviceIdType.MESH
 NT = (((1,), (1,)), ((), ()))
 NN = (((1,), (0,)), ((), ()))
@@ -62,8 +66,8 @@
     theta = math.pi * (np.arange(HALF) + 0.5) / NLAT
     weight = np.zeros(ROWS, np.float32)
     weight[:HALF] = math.pi / NLAT * (2.0 * math.pi / NLON) * np.sin(theta)
-    plain = np.zeros((MODES, ROWS, LANES), np.float32)
-    plain[:, :HALF, :MODES] = legendre_table(theta).transpose(0, 2, 1)
+    plain = np.zeros((ORDERS, ROWS, LANES), np.float32)
+    plain[:MODES, :HALF, :MODES] = legendre_table(theta).transpose(0, 2, 1)
     orders = np.arange(MODES)
     phase = orders[:, None] * np.arange(NLON)[None, :] % NLON
     angles = 2.0 * math.pi / NLON * phase
@@ -89,26 +93,28 @@
 
 def kernel(
     grid_dims,
-    scale,
     weight_ref,
     fields_ref,
     cot_ref,
     plain_hbm,
-    forward_ref,
-    inverse_ref,
+    forward_hbm,
+    inverse_hbm,
     real_ref,
     imag_ref,
-    out_real,
-    out_imag,
+    out_ref,
     field,
     cot,
     plain,
+    forward_ref,
+    inverse_ref,
     turned,
     work,
+    back_work,
     slope,
     spec,
     swap,
     filt,
+    mixes,
     acc,
     packed,
     xbuf,
@@ -172,8 +178,18 @@
     for target in everyone:
         pl.semaphore_signal(barrier, inc=1, device_id=target, device_id_type=MESH)
 
-    load = pltpu.make_async_copy(plain_hbm, plain, local_sem.at[0])
-    load.start()
+    loads = [
+        pltpu.make_async_copy(source, target, local_sem.at[index])
+        for index, (source, target) in enumerate(
+            (
+                (plain_hbm, plain),
+                (forward_hbm, forward_ref),
+                (inverse_hbm, inverse_ref),
+            )
+        )
+    ]
+    for load in loads:
+        load.start()
     mine_lanes = pl.ds(pl.multiple_of(me * SLICE, SLICE), SLICE)
     own_f = pltpu.make_async_copy(
         fields_ref.at[:, mine_lanes, :], field.at[pl.ds(me * BAND, BAND)], recv_f.at[me]
@@ -209,120 +225,154 @@
         block = target.at[pl.ds(band * BAND, BAND)]
         pltpu.make_async_copy(block, block, recv.at[band]).wait()
 
+    lane = lax.broadcasted_iota(jnp.int32, (LANES, LANES), 1)
+    degree = lax.broadcasted_iota(jnp.int32, (LANES, LANES), 0)
+    even_row = lax.rem(degree, 2) == lane // ROWS
     for index, source in enumerate((real_ref, imag_ref)):
-        filt[index] = jnp.zeros((LANES, LANES), jnp.float32)
+        acc[index] = jnp.zeros((LANES, LANES), jnp.float32)
         values = source[mine_lanes, :].astype(jnp.float32)
-        filt[index, :, :MODES] = jnp.concatenate([values] * 4, axis=0)
-        filt[index] = filt[index].T
+        acc[index, :, :MODES] = jnp.concatenate([values] * 4, axis=0)
+        values = acc[index].T
+        filt[0, index] = jnp.where(even_row, values, 0.0)
+        filt[1, index] = jnp.where(even_row, 0.0, values)
+    mixes[...] = jnp.zeros_like(mixes)
     work[pl.ds(HALF, LANES, stride=ROWS), :] = jnp.zeros((LANES, LANES), jnp.float32)
-    load.wait()
-
-    @pl.loop(0, MODES)
-    def _(m):
-        turned[m] = plain[m].astype(jnp.float32).T.astype(jnp.bfloat16)
+    for load in loads:
+        load.wait()
+
+    @pl.loop(0, ORDERS // 4)
+    def _(i):
+        for index in range(4):
+            turned[4 * i + index] = (
+                plain[4 * i + index].astype(jnp.float32).T.astype(jnp.bfloat16)
+            )
 
     zero = jnp.zeros((SLICE, NLON), jnp.bfloat16)
 
-    def to_modes(north, south, basis_ref, j, factor):
-        cosine = jnp.concatenate([north, zero, south, zero], axis=0)
-        sine = jnp.concatenate([zero, north, zero, south], axis=0)
-        modes = dot(basis_ref[0], cosine, NT) + dot(basis_ref[1], sine, NT)
-        if factor is not None:
-            modes = modes * factor
-        work[pl.ds(j, LANES, stride=ROWS), :] = modes
+    def to_modes(pairs, basis_ref, first, factors):
+        cosine = []
+        sine = []
+        for north, south in pairs:
+            even = (north + south).astype(jnp.bfloat16)
+            odd = (north - south).astype(jnp.bfloat16)
+            cosine += [even, zero, odd, zero]
+            sine += [zero, even, zero, odd]
+        modes = dot(basis_ref[0], jnp.concatenate(cosine, axis=0), NT)
+        modes += dot(basis_ref[1], jnp.concatenate(sine, axis=0), NT)
+        for index in range(len(pairs)):
+            part = modes[:, index * LANES : (index + 1) * LANES]
+            if factors is not None:
+                part = part * factors[index]
+            work[pl.ds(first + index, LANES, stride=ROWS), :] = part
 
     for band in (2, 1, 0):
         arrive(field, recv_f, band)
         arrive(field, recv_f, PARTS - 1 - band)
 
-        @pl.loop(0, BAND)
+        @pl.loop(0, BAND // STEP)
         def _(t, band=band):
-            j = band * BAND + t
+            first = band * BAND + t * STEP
+            js = [first + index for index in range(STEP)]
             to_modes(
-                field[j], field[NLAT - 1 - j], forward_ref, j, weight_ref[j]
+                [
+                    (
+                        field[j].astype(jnp.float32),
+                        field[NLAT - 1 - j].astype(jnp.float32),
+                    )
+                    for j in js
+                ],
+                forward_ref,
+                first,
+                [weight_ref[j] for j in js],
             )
 
-    lane = lax.broadcasted_iota(jnp.int32, (8, LANES), 1)
-    odd_group = (lax.rem(lane // SLICE, 2) == 1)[None]
-    degree = lax.broadcasted_iota(jnp.int32, (8, LANES), 0)
-    sign = (1 - 2 * lax.rem(degree, 2)).astype(jnp.float32)[None]
-
-    for group in range(8):
-        low = 16 * group
-        depth = LANES - low
-        pairs = (min(16, MODES - low)) // 2
-
-        @pl.loop(0, pairs)
-        def _(i, low=low, depth=depth):
-            for odd in (0, 1):
-                m = low + 2 * i + odd
-                at = pl.ds(pl.multiple_of(m * ROWS, ROWS), ROWS)
-                part = dot(turned[m, low:, :], work[at, :].astype(jnp.bfloat16))
-                other = pltpu.roll(part, 2 * SLICE, 1)
-                part = part.reshape(depth // 8, 8, LANES)
-                other = other.reshape(depth // 8, 8, LANES) * sign
-                full = part - other if odd else part + other
-                rounded = full.reshape(depth, LANES).astype(jnp.bfloat16)
-                values = rounded.astype(jnp.float32)
-                left = pltpu.roll(values, LANES - SLICE, 1).reshape(depth // 8, 8, LANES)
-                right = pltpu.roll(values, SLICE, 1).reshape(depth // 8, 8, LANES)
-                turn = jnp.where(odd_group, right, -left).reshape(depth, LANES)
-                spec[m, low:, :] = rounded
+    odd_group = lax.rem(lane[:ROWS] // SLICE, 2) == 1
+
+    def rows_of(m):
+        return pl.ds(pl.multiple_of(m * ROWS, ROWS), ROWS)
+
+    def synthesize(m, index):
+        back_work[rows_of(m), :] = dot(plain[m], mixes[index])
+
+    for low in range(0, ORDERS, 16):
+
+        @pl.loop(0, 16 // UNROLL)
+        def _(i, low=low):
+            start = low + UNROLL * i
+            for index in range(UNROLL):
+                synthesize(jnp.maximum(start - UNROLL, 0) + index, index)
+            for index in range(UNROLL):
+                m = start + index
+                modes = work[rows_of(m), :]
+                turn = jnp.where(
+                    odd_group,
+                    pltpu.roll(modes, SLICE, 1),
+                    -pltpu.roll(modes, LANES - SLICE, 1),
+                )
+                both = jnp.concatenate([modes, turn], axis=1).astype(jnp.bfloat16)
+                full = dot(turned[m, low:, :], both)
+                values, turn = full[:, :LANES], full[:, LANES:]
+                spec[m, low:, :] = values.astype(jnp.bfloat16)
                 swap[m, low:, :] = turn.astype(jnp.bfloat16)
-                mixed = values * filt[0, low:, :] + turn * filt[1, low:, :]
+                parity = index % 2
+                mixed = values * filt[parity, 0, low:, :] + turn * filt[parity, 1, low:, :]
                 mixed = mixed.astype(jnp.bfloat16)
                 if low:
                     mixed = jnp.concatenate(
                         [jnp.zeros((low, LANES), jnp.bfloat16), mixed], axis=0
                     )
-                work[at, :] = dot(plain[m], mixed)
-
-    @pl.loop(0, HALF)
-    def _(j):
-        modes = work[pl.ds(j, LANES, stride=ROWS), :].T.astype(jnp.bfloat16)
-        cosine = jnp.concatenate(
-            [modes[:SLICE], modes[2 * SLICE : 3 * SLICE]], axis=0
-        )
-        sine = jnp.concatenate([modes[SLICE : 2 * SLICE], modes[3 * SLICE :]], axis=0)
-        signal = dot(cosine, inverse_ref[0]) + dot(sine, inverse_ref[1])
-        slope[j] = gelu_slope(signal)
+                mixes[index] = mixed
+
+    for index in range(UNROLL):
+        synthesize(ORDERS - UNROLL + index, index)
+
+    @pl.loop(0, HALF // STEP)
+    def _(t):
+        for index in range(STEP):
+            j = t * STEP + index
+            modes = back_work[pl.ds(j, LANES, stride=ROWS), :].T
+            north = (modes[:ROWS] + modes[ROWS:]).astype(jnp.bfloat16)
+            south = (modes[:ROWS] - modes[ROWS:]).astype(jnp.bfloat16)
+            cosine = jnp.concatenate([north[:SLICE], south[:SLICE]], axis=0)
+            sine = jnp.concatenate([north[SLICE:], south[SLICE:]], axis=0)
+            signal = dot(
+                jnp.concatenate([cosine, sine], axis=1),
+                inverse_ref[...].reshape(2 * LANES, NLON),
+            )
+            slope[j] = gelu_slope(signal)
 
     for band in (2, 1, 0):
         arrive(cot, recv_c, band)
         arrive(cot, recv_c, PARTS - 1 - band)
 
-        @pl.loop(0, BAND)
+        @pl.loop(0, BAND // STEP)
         def _(t, band=band):
-            j = band * BAND + t
-            north = cot[j].astype(jnp.float32) * slope[j, :SLICE]
-            south = cot[NLAT - 1 - j].astype(jnp.float32) * slope[j, SLICE:]
-            to_modes(
-                north.astype(jnp.bfloat16),
-                south.astype(jnp.bfloat16),
-                inverse_ref,
-                j,
-                None,
-            )
+            first = band * BAND + t * STEP
+            pairs = []
+            for index in range(STEP):
+                j = first + index
+                north = cot[j].astype(jnp.float32) * slope[j, :SLICE]
+                south = cot[NLAT - 1 - j].astype(jnp.float32) * slope[j, SLICE:]
+                pairs.append((north, south))
+            to_modes(pairs, inverse_ref, first, None)
 
     acc[...] = jnp.zeros_like(acc)
-    for group in range(8):
-        low = 16 * group
-        pairs = (min(16, MODES - low)) // 2
-
-        @pl.loop(0, pairs)
+    for low in range(0, ORDERS, 16):
+
+        @pl.loop(0, 16 // BACK_UNROLL)
         def _(i, low=low):
-            total = [acc[0, low:, :], acc[1, low:, :]]
-            for odd in (0, 1):
-                m = low + 2 * i + odd
-                at = pl.ds(pl.multiple_of(m * ROWS, ROWS), ROWS)
-                back = dot(turned[m, low:, :], work[at, :].astype(jnp.bfloat16))
-                total[0] += back * spec[m, low:, :].astype(jnp.float32)
-                total[1] += back * swap[m, low:, :].astype(jnp.float32)
-            acc[0, low:, :] = total[0]
-            acc[1, low:, :] = total[1]
+            total = [acc[index, low:, :] for index in range(4)]
+            for index in range(BACK_UNROLL):
+                m = low + BACK_UNROLL * i + index
+                parity = index % 2
+                back = dot(turned[m, low:, :], work[rows_of(m), :].astype(jnp.bfloat16))
+                total[parity] += back * spec[m, low:, :].astype(jnp.float32)
+                total[2 + parity] += back * swap[m, low:, :].astype(jnp.float32)
+            for index in range(4):
+                acc[index, low:, :] = total[index]
 
     for index in range(2):
-        total = acc[index].T * scale
+        total = jnp.where(even_row, acc[2 * index], acc[2 * index + 1]).T
         packed[pl.ds(index * SLICE, SLICE), :] = (
             total[:SLICE] + total[SLICE : 2 * SLICE]
         ) + (total[2 * SLICE : 3 * SLICE] + total[3 * SLICE :])
@@ -393,8 +443,10 @@
         pltpu.make_async_copy(spot, spot, recv_g.at[x]).wait()
 
     for s in range(PARTS):
-        out_real[s * SLICE : (s + 1) * SLICE, :] = gathered[s, :SLICE, :MODES]
-        out_imag[s * SLICE : (s + 1) * SLICE, :] = gathered[s, SLICE:, :MODES]
+        for index in range(2):
+            out_ref[index, s * SLICE : (s + 1) * SLICE, :] = gathered[
+                s, index * SLICE : (index + 1) * SLICE, :MODES
+            ]
     for copy in sends:
         copy.wait_send()
 
@@ -407,40 +459,44 @@
     cotangent = jnp.transpose(cotangent[0], (0, 2, 1))
     vmem = pl.BlockSpec(memory_space=pltpu.VMEM)
     anywhere = pl.BlockSpec(memory_space=pl.ANY)
-    out = jax.ShapeDtypeStruct((CHANNELS, MODES), jnp.float32)
+    out = jax.ShapeDtypeStruct((2, CHANNELS, MODES), jnp.float32)
     dma = pltpu.SemaphoreType.DMA
     result = pl.pallas_call(
-        functools.partial(kernel, grid_dims, 1.0 / batch),
-        out_shape=(out, out),
+        functools.partial(kernel, grid_dims),
+        out_shape=out,
         in_specs=[
             pl.BlockSpec(memory_space=pltpu.SMEM),
             anywhere,
             anywhere,
             anywhere,
-            vmem,
-            vmem,
+            anywhere,
+            anywhere,
             vmem,
             vmem,
         ],
-        out_specs=(vmem, vmem),
+        out_specs=vmem,
         scratch_shapes=[
             pltpu.VMEM((NLAT, SLICE, NLON), jnp.bfloat16),
             pltpu.VMEM((NLAT, SLICE, NLON), jnp.bfloat16),
-            pltpu.VMEM((MODES, ROWS, LANES), jnp.bfloat16),
-            pltpu.VMEM((MODES, LANES, ROWS), jnp.bfloat16),
-            pltpu.VMEM((LANES * ROWS, LANES), jnp.float32),
+            pltpu.VMEM((ORDERS, ROWS, LANES), jnp.bfloat16),
+            pltpu.VMEM((2, LANES, NLON), jnp.bfloat16),
+            pltpu.VMEM((2, LANES, NLON), jnp.bfloat16),
+            pltpu.VMEM((ORDERS, LANES, ROWS), jnp.bfloat16),
+            pltpu.VMEM((ORDERS * ROWS, LANES), jnp.float32),
+            pltpu.VMEM((ORDERS * ROWS, LANES), jnp.float32),
             pltpu.VMEM((HALF, ROWS, NLON), jnp.float32),
-            pltpu.VMEM((MODES, LANES, LANES), jnp.bfloat16),
-            pltpu.VMEM((MODES, LANES, LANES), jnp.bfloat16),
-            pltpu.VMEM((2, LANES, LANES), jnp.float32),
-            pltpu.VMEM((2, LANES, LANES), jnp.float32),
+            pltpu.VMEM((ORDERS, LANES, LANES), jnp.bfloat16),
+            pltpu.VMEM((ORDERS, LANES, LANES), jnp.bfloat16),
+            pltpu.VMEM((2, 2, LANES, LANES), jnp.float32),
+            pltpu.VMEM((UNROLL, LANES, LANES), jnp.bfloat16),
+            pltpu.VMEM((4, LANES, LANES), jnp.float32),
             pltpu.VMEM((ROWS, LANES), jnp.float32),
             pltpu.VMEM((n_x, rows, LANES), jnp.float32),
             pltpu.VMEM((n_y, rows, LANES), jnp.float32),
             pltpu.VMEM((n_z, rows, LANES), jnp.float32),
             pltpu.VMEM((3, rows, LANES), jnp.float32),
             pltpu.VMEM((PARTS, ROWS, LANES), jnp.float32),
-            dma((1,)),
+            dma((3,)),
             dma((PARTS,)),
             dma((PARTS,)),
             dma((PARTS,)),
@@ -469,6 +525,7 @@
         spec_real.T,
         spec_imag.T,
     )
+    result = result * (1.0 / batch)
     return (result[0].T, result[1].T)
 
 

time: 164 us -> 117 us (0.71)
  Pallas kernels: 160 us -> 115 us
  local copies, waits for them, and re-layouts: 3.08 us -> 0.69 us
    pallas_call x1, Pallas kernels: 160 us -> 115 us  [on_device(): pl.pallas_call(functools.partial(kernel, grid_dims), out_shape=out, in_sp...]
    unnamed x2 -> x0, local copies, waits for them, and re-layouts: 3.08 us -> none
where the time goes in v2:
time: 117 us
  Pallas kernels  115 us (98%)
    pallas_call x1, Pallas kernels, on_device(): pl.pallas_call(functools.partial(kernel, grid_dims), out_shape=out, in_sp...  115 us

profile of v2, /device:TPU:1, one launch (start us, length us, event | category | flops | bytes accessed | tf_op | source)
XLA Modules:
  0.0 116.8 jit_solution(10386765735694780857)
XLA Ops:
  0.6 114.5 %shard_map.95 = f32[2,192,126]{2,1,0:T(8,128)} custom-call(f32[64]{0:T(128)} %constant.10.clone.weight_ref, bf16[21,192,252]{2,1,0:T(8,128)(2,1)} %bitcast.16, bf16[21,192,252]{2,1,0:T(8,128)(2,1)} %bitcast.17, bf16[128,64,128]{2,1,0:T(8,128)(2,1)} %constant.11.clone.plain_hbm, bf16[2,128,252]{2,1,0:T(8,128)(2,1)} %constant.12.clone.forward_hbm, ...), custom_call_target="tpu_custom_call" | custom-call | tf_op jit(solution)/shard_map/pallas_call | solution.py:464
  115.2 0.9 broadcast_multiply_fusion
  116.1 0.7 slice_bitcast_fusion

commit v3 on v2

--- a/solution.py
+++ b/solution.py
@@ -64,8 +64,8 @@
 
 def tables():
     theta = math.pi * (np.arange(HALF) + 0.5) / NLAT
-    weight = np.zeros(ROWS, np.float32)
-    weight[:HALF] = math.pi / NLAT * (2.0 * math.pi / NLON) * np.sin(theta)
+    weight = np.zeros((ROWS, LANES), np.float32)
+    weight[:HALF] = (math.pi / NLAT * (2.0 * math.pi / NLON) * np.sin(theta))[:, None]
     plain = np.zeros((ORDERS, ROWS, LANES), np.float32)
     plain[:MODES, :HALF, :MODES] = legendre_table(theta).transpose(0, 2, 1)
     orders = np.arange(MODES)
@@ -93,20 +93,24 @@
 
 def kernel(
     grid_dims,
-    weight_ref,
+    scale,
+    weight_hbm,
     fields_ref,
     cot_ref,
     plain_hbm,
     forward_hbm,
     inverse_hbm,
-    real_ref,
-    imag_ref,
+    real_hbm,
+    imag_hbm,
     out_ref,
     field,
     cot,
     plain,
     forward_ref,
     inverse_ref,
+    weight_ref,
+    real_ref,
+    imag_ref,
     turned,
     work,
     back_work,
@@ -146,15 +150,20 @@
     xi = lax.rem(dp // n_y, n_x)
     yi = lax.rem(dp, n_y)
     chip, core = me // 2, lax.rem(me, 2)
-    first = jnp.where(chip == 0, 2, 0)
-    second = 3 - chip - first
+    near = jnp.where(chip == 1, 0, 1)
+    far = 3 - chip - near
     space_peers = [
-        2 * first + core,
-        2 * first + 1 - core,
-        2 * second + core,
-        2 * second + 1 - core,
         2 * chip + 1 - core,
-    ]
+        2 * near + core,
+        2 * near + 1 - core,
+        2 * far + core,
+        2 * far + 1 - core,
+    ]
+    second = jnp.where(chip == 0, 1 - core, jnp.where(chip == 2, core, 1))
+
+    def band_of(turn):
+        return jnp.where(turn == 0, 2, jnp.where(turn == 1, second, 1 - second))
+
     x_peers = [lax.rem(xi + r, n_x) for r in range(1, n_x)]
     y_peers = [lax.rem(yi + r, n_y) for r in range(1, n_y)]
     z_peers = [lax.rem(zi + r, n_z) for r in range(1, n_z)]
@@ -185,6 +194,9 @@
                 (plain_hbm, plain),
                 (forward_hbm, forward_ref),
                 (inverse_hbm, inverse_ref),
+                (weight_hbm, weight_ref),
+                (real_hbm, real_ref),
+                (imag_hbm, imag_ref),
             )
         )
     ]
@@ -225,6 +237,9 @@
         block = target.at[pl.ds(band * BAND, BAND)]
         pltpu.make_async_copy(block, block, recv.at[band]).wait()
 
+    for load in loads:
+        load.wait()
+
     lane = lax.broadcasted_iota(jnp.int32, (LANES, LANES), 1)
     degree = lax.broadcasted_iota(jnp.int32, (LANES, LANES), 0)
     even_row = lax.rem(degree, 2) == lane // ROWS
@@ -237,9 +252,6 @@
         filt[1, index] = jnp.where(even_row, 0.0, values)
     mixes[...] = jnp.zeros_like(mixes)
     work[pl.ds(HALF, LANES, stride=ROWS), :] = jnp.zeros((LANES, LANES), jnp.float32)
-    for load in loads:
-        load.wait()
-
     @pl.loop(0, ORDERS // 4)
     def _(i):
         for index in range(4):
@@ -265,12 +277,14 @@
                 part = part * factors[index]
             work[pl.ds(first + index, LANES, stride=ROWS), :] = part
 
-    for band in (2, 1, 0):
+    @pl.loop(0, PARTS // 2)
+    def _(turn):
+        band = band_of(turn)
         arrive(field, recv_f, band)
         arrive(field, recv_f, PARTS - 1 - band)
 
         @pl.loop(0, BAND // STEP)
-        def _(t, band=band):
+        def _(t):
             first = band * BAND + t * STEP
             js = [first + index for index in range(STEP)]
             to_modes(
@@ -283,7 +297,7 @@
                 ],
                 forward_ref,
                 first,
-                [weight_ref[j] for j in js],
+                [weight_ref[pl.ds(j, 1), :] for j in js],
             )
 
     odd_group = lax.rem(lane[:ROWS] // SLICE, 2) == 1
@@ -341,12 +355,14 @@
             )
             slope[j] = gelu_slope(signal)
 
-    for band in (2, 1, 0):
+    @pl.loop(0, PARTS // 2)
+    def _(turn):
+        band = band_of(turn)
         arrive(cot, recv_c, band)
         arrive(cot, recv_c, PARTS - 1 - band)
 
         @pl.loop(0, BAND // STEP)
-        def _(t, band=band):
+        def _(t):
             first = band * BAND + t * STEP
             pairs = []
             for index in range(STEP):
@@ -372,7 +388,7 @@
                 acc[index, low:, :] = total[index]
 
     for index in range(2):
-        total = jnp.where(even_row, acc[2 * index], acc[2 * index + 1]).T
+        total = jnp.where(even_row, acc[2 * index], acc[2 * index + 1]).T * scale
         packed[pl.ds(index * SLICE, SLICE), :] = (
             total[:SLICE] + total[SLICE : 2 * SLICE]
         ) + (total[2 * SLICE : 3 * SLICE] + total[3 * SLICE :])
@@ -462,18 +478,12 @@
     out = jax.ShapeDtypeStruct((2, CHANNELS, MODES), jnp.float32)
     dma = pltpu.SemaphoreType.DMA
     result = pl.pallas_call(
-        functools.partial(kernel, grid_dims),
+        functools.partial(kernel, grid_dims, 1.0 / batch),
         out_shape=out,
         in_specs=[
-            pl.BlockSpec(memory_space=pltpu.SMEM),
             anywhere,
-            anywhere,
-            anywhere,
-            anywhere,
-            anywhere,
-            vmem,
-            vmem,
-        ],
+        ]
+        * 8,
         out_specs=vmem,
         scratch_shapes=[
             pltpu.VMEM((NLAT, SLICE, NLON), jnp.bfloat16),
@@ -481,6 +491,9 @@
             pltpu.VMEM((ORDERS, ROWS, LANES), jnp.bfloat16),
             pltpu.VMEM((2, LANES, NLON), jnp.bfloat16),
             pltpu.VMEM((2, LANES, NLON), jnp.bfloat16),
+            pltpu.VMEM((ROWS, LANES), jnp.float32),
+            pltpu.VMEM((CHANNELS, MODES), jnp.bfloat16),
+            pltpu.VMEM((CHANNELS, MODES), jnp.bfloat16),
             pltpu.VMEM((ORDERS, LANES, ROWS), jnp.bfloat16),
             pltpu.VMEM((ORDERS * ROWS, LANES), jnp.float32),
             pltpu.VMEM((ORDERS * ROWS, LANES), jnp.float32),
@@ -496,7 +509,7 @@
             pltpu.VMEM((n_z, rows, LANES), jnp.float32),
             pltpu.VMEM((3, rows, LANES), jnp.float32),
             pltpu.VMEM((PARTS, ROWS, LANES), jnp.float32),
-            dma((3,)),
+            dma((6,)),
             dma((PARTS,)),
             dma((PARTS,)),
             dma((PARTS,)),
@@ -525,7 +538,6 @@
         spec_real.T,
         spec_imag.T,
     )
-    result = result * (1.0 / batch)
     return (result[0].T, result[1].T)
 
 

time: 117 us -> 111 us (0.949)
  Pallas kernels: 115 us -> 109 us
    pallas_call x1, Pallas kernels: 115 us -> 109 us  [on_device(): pl.pallas_call(functools.partial(kernel, grid_dims, 1.0 / batch), out_sha...]
where the time goes in v3:
time: 111 us
  Pallas kernels  109 us (98%)
  local copies, waits for them, and re-layouts  1.63 us (1%)
    pallas_call x1, Pallas kernels, on_device(): pl.pallas_call(functools.partial(kernel, grid_dims, 1.0 / batch), out_sha...  109 us

profile of v3, /device:TPU:1, one launch (start us, length us, event | category | flops | bytes accessed | tf_op | source)
XLA Modules:
  0.0 111.0 jit_solution(15063474917017617992)
XLA Ops:
  0.6 108.7 %shard_map.95 = f32[2,192,126]{2,1,0:T(8,128)} custom-call(f32[64,128]{1,0:T(8,128)} %constant.8.clone.weight_hbm, bf16[21,192,252]{2,1,0:T(8,128)(2,1)} %bitcast.16, bf16[21,192,252]{2,1,0:T(8,128)(2,1)} %bitcast.17, bf16[128,64,128]{2,1,0:T(8,128)(2,1)} %constant.9.clone.plain_hbm, bf16[2,128,252]{2,1,0:T(8,128)(2,1)} %constant.10.clone.forward_hbm, ...), custom_call_target="tpu_custom_call" | custom-call | tf_op jit(solution)/shard_map/pallas_call | solution.py:480
  109.4 1.6 %slice_bitcast_fusion = (f32[126,192]{0,1:T(8,128)}, f32[126,192]{0,1:T(8,128)}) fusion(f32[2,192,126]{2,1,0:T(8,128)} %shard_map.95), kind=kLoop, calls=%fused_computation | loop fusion | bytes 387072 | tf_op jit(solution)/shard_map/transpose | solution.py:541

commit v4 on v3

--- a/solution.py
+++ b/solution.py
@@ -22,8 +22,10 @@
 ROWS = 64
 LANES = 128
 STEP = 3
+PIECES = ((0, 9), (9, 6), (15, 6))
 UNROLL = 4
-BACK_UNROLL = 8
+BACK_UNROLL = 16
+DEGREES = 64
 MESH = pl.DeviceIdType.MESH
 NT = (((1,), (1,)), ((), ()))
 NN = (((1,), (0,)), ((), ()))
@@ -206,11 +208,24 @@
     own_f = pltpu.make_async_copy(
         fields_ref.at[:, mine_lanes, :], field.at[pl.ds(me * BAND, BAND)], recv_f.at[me]
     )
-    own_c = pltpu.make_async_copy(
-        cot_ref.at[:, mine_lanes, :], cot.at[pl.ds(me * BAND, BAND)], recv_c.at[me]
-    )
+
+    def offset(band, piece):
+        start, size = PIECES[piece]
+        return jnp.where(band < PARTS // 2, start, BAND - start - size)
+
+    own_c = []
+    for piece, (_, size) in enumerate(PIECES):
+        start = offset(me, piece)
+        own_c.append(
+            pltpu.make_async_copy(
+                cot_ref.at[pl.ds(start, size), mine_lanes, :],
+                cot.at[pl.ds(me * BAND + start, size)],
+                recv_c.at[me, piece],
+            )
+        )
     own_f.start()
-    own_c.start()
+    for copy in own_c:
+        copy.start()
     pl.semaphore_wait(barrier, len(everyone))
 
     def exchange(source, target, send, recv):
@@ -231,7 +246,21 @@
         return copies
 
     sends = exchange(fields_ref, field, send_f, recv_f)
-    sends += exchange(cot_ref, cot, send_c, recv_c)
+    for slot, peer in enumerate(space_peers):
+        lanes = pl.ds(pl.multiple_of(peer * SLICE, SLICE), SLICE)
+        for piece, (_, size) in enumerate(PIECES):
+            start = offset(me, piece)
+            sends.append(
+                pltpu.make_async_remote_copy(
+                    src_ref=cot_ref.at[pl.ds(start, size), lanes, :],
+                    dst_ref=cot.at[pl.ds(me * BAND + start, size)],
+                    send_sem=send_c.at[slot, piece],
+                    recv_sem=recv_c.at[me, piece],
+                    device_id={"space": peer},
+                    device_id_type=MESH,
+                )
+            )
+            sends[-1].start()
 
     def arrive(target, recv, band):
         block = target.at[pl.ds(band * BAND, BAND)]
@@ -326,9 +355,10 @@
                 both = jnp.concatenate([modes, turn], axis=1).astype(jnp.bfloat16)
                 full = dot(turned[m, low:, :], both)
                 values, turn = full[:, :LANES], full[:, LANES:]
-                spec[m, low:, :] = values.astype(jnp.bfloat16)
-                swap[m, low:, :] = turn.astype(jnp.bfloat16)
                 parity = index % 2
+                keep = even_row[low:] if parity == 0 else jnp.logical_not(even_row[low:])
+                spec[m, low:, :] = jnp.where(keep, values, 0.0).astype(jnp.bfloat16)
+                swap[m, low:, :] = jnp.where(keep, turn, 0.0).astype(jnp.bfloat16)
                 mixed = values * filt[parity, 0, low:, :] + turn * filt[parity, 1, low:, :]
                 mixed = mixed.astype(jnp.bfloat16)
                 if low:
@@ -358,37 +388,45 @@
     @pl.loop(0, PARTS // 2)
     def _(turn):
         band = band_of(turn)
-        arrive(cot, recv_c, band)
-        arrive(cot, recv_c, PARTS - 1 - band)
-
-        @pl.loop(0, BAND // STEP)
-        def _(t):
-            first = band * BAND + t * STEP
-            pairs = []
-            for index in range(STEP):
-                j = first + index
-                north = cot[j].astype(jnp.float32) * slope[j, :SLICE]
-                south = cot[NLAT - 1 - j].astype(jnp.float32) * slope[j, SLICE:]
-                pairs.append((north, south))
-            to_modes(pairs, inverse_ref, first, None)
+        for piece, (begin, size) in enumerate(PIECES):
+            for side in (band, PARTS - 1 - band):
+                block = cot.at[pl.ds(side * BAND + offset(side, piece), size)]
+                pltpu.make_async_copy(block, block, recv_c.at[side, piece]).wait()
+
+            @pl.loop(0, size // STEP)
+            def _(t, begin=begin):
+                first = band * BAND + begin + t * STEP
+                pairs = []
+                for index in range(STEP):
+                    j = first + index
+                    north = cot[j].astype(jnp.float32) * slope[j, :SLICE]
+                    south = cot[NLAT - 1 - j].astype(jnp.float32) * slope[j, SLICE:]
+                    pairs.append((north, south))
+                to_modes(pairs, inverse_ref, first, None)
 
     acc[...] = jnp.zeros_like(acc)
     for low in range(0, ORDERS, 16):
+        spans = [
+            (max(low, start), start + DEGREES)
+            for start in range(0, ORDERS, DEGREES)
+            if start + DEGREES > low
+        ]
 
         @pl.loop(0, 16 // BACK_UNROLL)
-        def _(i, low=low):
-            total = [acc[index, low:, :] for index in range(4)]
-            for index in range(BACK_UNROLL):
-                m = low + BACK_UNROLL * i + index
-                parity = index % 2
-                back = dot(turned[m, low:, :], work[rows_of(m), :].astype(jnp.bfloat16))
-                total[parity] += back * spec[m, low:, :].astype(jnp.float32)
-                total[2 + parity] += back * swap[m, low:, :].astype(jnp.float32)
-            for index in range(4):
-                acc[index, low:, :] = total[index]
+        def _(i, low=low, spans=spans):
+            for begin, end in spans:
+                total = [acc[0, begin:end, :], acc[1, begin:end, :]]
+                for index in range(BACK_UNROLL):
+                    m = low + BACK_UNROLL * i + index
+                    modes = work[rows_of(m), :].astype(jnp.bfloat16)
+                    back = dot(turned[m, begin:end, :], modes)
+                    total[0] += back * spec[m, begin:end, :].astype(jnp.float32)
+                    total[1] += back * swap[m, begin:end, :].astype(jnp.float32)
+                acc[0, begin:end, :] = total[0]
+                acc[1, begin:end, :] = total[1]
 
     for index in range(2):
-        total = jnp.where(even_row, acc[2 * index], acc[2 * index + 1]).T * scale
+        total = acc[index].T * scale
         packed[pl.ds(index * SLICE, SLICE), :] = (
             total[:SLICE] + total[SLICE : 2 * SLICE]
         ) + (total[2 * SLICE : 3 * SLICE] + total[3 * SLICE :])
@@ -502,7 +540,7 @@
             pltpu.VMEM((ORDERS, LANES, LANES), jnp.bfloat16),
             pltpu.VMEM((2, 2, LANES, LANES), jnp.float32),
             pltpu.VMEM((UNROLL, LANES, LANES), jnp.bfloat16),
-            pltpu.VMEM((4, LANES, LANES), jnp.float32),
+            pltpu.VMEM((2, LANES, LANES), jnp.float32),
             pltpu.VMEM((ROWS, LANES), jnp.float32),
             pltpu.VMEM((n_x, rows, LANES), jnp.float32),
             pltpu.VMEM((n_y, rows, LANES), jnp.float32),
@@ -512,8 +550,8 @@
             dma((6,)),
             dma((PARTS,)),
             dma((PARTS,)),
-            dma((PARTS,)),
-            dma((PARTS,)),
+            dma((PARTS, len(PIECES))),
+            dma((PARTS, len(PIECES))),
             dma((n_x,)),
             dma((n_x,)),
             dma((n_y,)),

time: 111 us -> 107 us (0.964)
  Pallas kernels: 109 us -> 105 us
    pallas_call x1, Pallas kernels: 109 us -> 105 us  [on_device(): pl.pallas_call(functools.partial(kernel, grid_dims, 1.0 / batch), out_sha...]
where the time goes in v4:
time: 107 us
  Pallas kernels  105 us (98%)
  local copies, waits for them, and re-layouts  1.63 us (2%)
    pallas_call x1, Pallas kernels, on_device(): pl.pallas_call(functools.partial(kernel, grid_dims, 1.0 / batch), out_sha...  105 us

profile of v4, /device:TPU:1, one launch (start us, length us, event | category | flops | bytes accessed | tf_op | source)
XLA Modules:
  0.0 106.9 jit_solution(10235994828635879797)
XLA Ops:
  0.6 104.6 %shard_map.95 = f32[2,192,126]{2,1,0:T(8,128)} custom-call(f32[64,128]{1,0:T(8,128)} %constant.8.clone.weight_hbm, bf16[21,192,252]{2,1,0:T(8,128)(2,1)} %bitcast.16, bf16[21,192,252]{2,1,0:T(8,128)(2,1)} %bitcast.17, bf16[128,64,128]{2,1,0:T(8,128)(2,1)} %constant.9.clone.plain_hbm, bf16[2,128,252]{2,1,0:T(8,128)(2,1)} %constant.10.clone.forward_hbm, ...), custom_call_target="tpu_custom_call" | custom-call | tf_op jit(solution)/shard_map/pallas_call | solution.py:518
  105.3 1.6 %slice_bitcast_fusion = (f32[126,192]{0,1:T(8,128)}, f32[126,192]{0,1:T(8,128)}) fusion(f32[2,192,126]{2,1,0:T(8,128)} %shard_map.95), kind=kLoop, calls=%fused_computation | loop fusion | bytes 387072 | tf_op jit(solution)/shard_map/transpose | solution.py:579

commit v5 on v4

--- a/solution.py
+++ b/solution.py
@@ -22,7 +22,7 @@
 ROWS = 64
 LANES = 128
 STEP = 3
-PIECES = ((0, 9), (9, 6), (15, 6))
+PIECES = ((0, 9), (9, 6), (15, 3), (18, 3))
 UNROLL = 4
 BACK_UNROLL = 16
 DEGREES = 64
@@ -127,6 +127,7 @@
     ybuf,
     zbuf,
     mine,
+    final,
     gathered,
     local_sem,
     send_f,
@@ -471,14 +472,14 @@
     zbuf[zi] = mine[1]
     for copy in copies:
         copy.wait()
-    mine[2] = sum((zbuf[i] for i in range(1, n_z)), zbuf[0])
+    final[...] = sum((zbuf[i] for i in range(1, n_z)), zbuf[0]).astype(jnp.bfloat16)
 
     spot = gathered.at[me, piece(xi)]
     copies = [
-        remote(mine.at[2], spot, send_s.at[r], recv_s.at[me], {"space": s})
+        remote(final, spot, send_s.at[r], recv_s.at[me], {"space": s})
         for r, s in enumerate(space_peers)
     ]
-    gathered[me, piece(xi)] = mine[2]
+    gathered[me, piece(xi)] = final[...]
     for copy in copies:
         copy.wait_send()
     for s in space_peers:
@@ -500,7 +501,7 @@
         for index in range(2):
             out_ref[index, s * SLICE : (s + 1) * SLICE, :] = gathered[
                 s, index * SLICE : (index + 1) * SLICE, :MODES
-            ]
+            ].astype(jnp.float32)
     for copy in sends:
         copy.wait_send()
 
@@ -545,8 +546,9 @@
             pltpu.VMEM((n_x, rows, LANES), jnp.float32),
             pltpu.VMEM((n_y, rows, LANES), jnp.float32),
             pltpu.VMEM((n_z, rows, LANES), jnp.float32),
-            pltpu.VMEM((3, rows, LANES), jnp.float32),
-            pltpu.VMEM((PARTS, ROWS, LANES), jnp.float32),
+            pltpu.VMEM((2, rows, LANES), jnp.float32),
+            pltpu.VMEM((rows, LANES), jnp.bfloat16),
+            pltpu.VMEM((PARTS, ROWS, LANES), jnp.bfloat16),
             dma((6,)),
             dma((PARTS,)),
             dma((PARTS,)),

time: 107 us -> 106 us (level)
  no operation moved by 1% of the time
where the time goes in v5:
time: 106 us
  Pallas kernels  104 us (98%)
  local copies, waits for them, and re-layouts  1.63 us (2%)
    pallas_call x1, Pallas kernels, on_device(): pl.pallas_call(functools.partial(kernel, grid_dims, 1.0 / batch), out_sha...  104 us

profile of v5, /device:TPU:1, one launch (start us, length us, event | category | flops | bytes accessed | tf_op | source)
XLA Modules:
  0.0 106.0 jit_solution(844721379244076842)
XLA Ops:
  0.6 103.7 %shard_map.95 = f32[2,192,126]{2,1,0:T(8,128)} custom-call(f32[64,128]{1,0:T(8,128)} %constant.8.clone.weight_hbm, bf16[21,192,252]{2,1,0:T(8,128)(2,1)} %bitcast.16, bf16[21,192,252]{2,1,0:T(8,128)(2,1)} %bitcast.17, bf16[128,64,128]{2,1,0:T(8,128)(2,1)} %constant.9.clone.plain_hbm, bf16[2,128,252]{2,1,0:T(8,128)(2,1)} %constant.10.clone.forward_hbm, ...), custom_call_target="tpu_custom_call" | custom-call | tf_op jit(solution)/shard_map/pallas_call | solution.py:519
  104.4 1.6 %slice_bitcast_fusion = (f32[126,192]{0,1:T(8,128)}, f32[126,192]{0,1:T(8,128)}) fusion(f32[2,192,126]{2,1,0:T(8,128)} %shard_map.95), kind=kLoop, calls=%fused_computation | loop fusion | bytes 387072 | tf_op jit(solution)/shard_map/transpose | solution.py:581
